TPU v7x, 256 devices: a whole 4x4x8 slice. The times are simulated.
256 devices in a mesh: dp: 2 (over core), seq: 128 (over z, y, x).
Axes of the slice: x: 4, y: 4, z: 8, core: 2. Of those that a mesh axis runs over, the one named last changes fastest.
Arguments:
- joints_x: bfloat16 [2, 256, 128, 1536], P('dp', 'seq'), may hold values from -6 to 6
- cotangent: bfloat16 [2, 256, 128, 1536], P('dp', 'seq'), may hold values from -6 to 6
- hidden: int32 [2, 256, 128], P('dp', 'seq'), may hold values 0 or 1
- stream_clip: int32 [2, 256], P('dp'), may hold values from 0 to 271, as said below
- stream_kind: int32 [2, 256], P('dp'), may hold values from 0 to 3, as said below
- adjacency: int32 [4, 136, 136], replicated, may hold values 0 or 1
- mask_token: bfloat16 [1536], replicated, may hold values from -6 to 6
- norm_gain: float32 [1536], replicated, may hold values from 0.1 to 1.9
- w_qkv: bfloat16 [1536, 2304], replicated, may hold values from -0.15625 to 0.15625
- w_out: bfloat16 [768, 1536], replicated, may hold values from -0.21875 to 0.21875
- graph_coef: float32 [12], replicated, may hold values from 0.5 to 260
Outputs:
- layer_out: bfloat16 [2, 256, 128, 1536], P('dp', 'seq')
- grad_x: bfloat16 [2, 256, 128, 1536], P('dp', 'seq')
- grad_token: float32 [1536], replicated
- grad_gain: float32 [1536], replicated
- grad_coef: float32 [12], replicated
Inputs may be any that keep to these rules, and one draw needn't show every extreme that they name: `stream_clip`: the slots of a clip are consecutive, clip numbers rise in slot order, starting at 0, at most 16 of them; every slot after the last clip, the last slot always among them, is padding numbered 16 plus its slot index. `stream_kind`: constant within a clip; a clip of kind 0, 1, 2, 3 has 17, 25, 52, 133 slots; slot 0 starts a clip of kind 3; padding slots have kind 0.
All inputs are finite; a program needn't handle non-finite values. No bound on the sum of `hidden` on one device may be relied on, other than what follows from the above.
Results may differ from a plain program's by a relative error of at most 0.0089.
Values may be sent and summed in bfloat16 or wider, within the bound.
A program may use at most 128 MiB of HBM per device.

v0:
```python
import functools

import jax
import jax.numpy as jnp
from jax import lax
from jax.experimental import pallas as pl
from jax.experimental.pallas import tpu as pltpu
from jax.sharding import PartitionSpec as P

MESH = pl.DeviceIdType.MESH
BF = jnp.bfloat16
F32 = jnp.float32
NSEQ = 128
XY = 16
NZ = 8
D = 1536
HW = 768
HEADS = 12
HD = 64
R = 256
L = 128
KINDS = 4
JM = 136
PAIRS = HEADS // 2


def iota(shape, axis):
    return lax.broadcasted_iota(jnp.int32, shape, axis)


def nn(a, b):
    return jnp.dot(a, b, preferred_element_type=F32)


def nt(a, b):
    return lax.dot_general(a, b, (((1,), (1,)), ((), ())), preferred_element_type=F32)


def to_column(row, n):
    diag = iota((n, n), 0) == iota((n, n), 1)
    return jnp.sum(jnp.where(diag, row, jnp.zeros_like(row)), axis=1, keepdims=True)


def fused_kernel(
    x_hbm,
    cot_hbm,
    hid_hbm,
    clip_hbm,
    kind_hbm,
    adj_hbm,
    tok_hbm,
    gain_hbm,
    wqkv_hbm,
    wout_hbm,
    coef_ref,
    out_hbm,
    gx_hbm,
    token_ref,
    gain_out_ref,
    coef_out_ref,
    xv,
    cotv,
    hidv,
    clipv,
    kindv,
    adjv,
    tokv,
    gainv,
    wq,
    wo,
    outv,
    gxv,
    xs,
    xr,
    gs,
    gr,
    cs,
    cr,
    ns,
    nr,
    hcol,
    rcol,
    qkv,
    xn,
    gc,
    vt,
    kt,
    ctt,
    pts,
    du,
    link,
    neg,
    coefs,
    tmp,
    a0,
    b1,
    b2,
    b3,
    in_sem,
    send_sem,
    recv_sem,
    loc_sem,
    out_sem,
):
    me = lax.axis_index("seq")
    core = lax.axis_index("dp")
    z = me // XY
    yx = me % XY
    y = yx // 4
    x = yx % 4

    loads = [
        (x_hbm.at[0], xv),
        (hid_hbm, hidv),
        (tok_hbm, tokv),
        (gain_hbm, gainv),
        (cot_hbm.at[0], cotv),
        (wout_hbm, wo),
        (clip_hbm, clipv),
        (kind_hbm, kindv),
        (adj_hbm, adjv),
        (wqkv_hbm, wq),
    ]
    load = [pltpu.make_async_copy(s, d, in_sem.at[i]) for i, (s, d) in enumerate(loads)]
    for c in load:
        c.start()

    barrier = pltpu.get_barrier_semaphore()

    def greet(k, _):
        pl.semaphore_signal(
            barrier, inc=1, device_id={"seq": (me + k) % NSEQ}, device_id_type=MESH
        )
        return 0

    lax.fori_loop(1, NSEQ, greet, 0)

    def greet_other(k, _):
        pl.semaphore_signal(
            barrier,
            inc=1,
            device_id={"dp": 1 - core, "seq": k * XY + yx},
            device_id_type=MESH,
        )
        return 0

    lax.fori_loop(0, NZ, greet_other, 0)

    for c in load[:4]:
        c.wait()
    tok = tokv[...].astype(F32)
    gain = gainv[...]
    hid = hidv[0].astype(F32)
    for s in range(2):
        hcol[s] = to_column(hid[s : s + 1, :], L)
    pl.semaphore_wait(barrier, NSEQ - 1 + NZ)

    def peer(dz, dyx):
        return ((z + dz) % NZ) * XY + ((y + dyx // 4) % 4) * 4 + (x + dyx % 4) % 4

    def send(src, dst, phase, to):
        return pltpu.make_async_remote_copy(
            src_ref=src,
            dst_ref=dst,
            send_sem=send_sem.at[phase],
            recv_sem=recv_sem.at[phase],
            device_id={"seq": to},
            device_id_type=MESH,
        )

    def send_all(src, dst, phase):
        pltpu.make_async_copy(src.at[me], dst.at[me], loc_sem.at[phase]).start()

        def body(k, _):
            to = peer(k % NZ, k // NZ)
            send(src.at[to], dst.at[me], phase, to).start()
            return 0

        lax.fori_loop(1, NSEQ, body, 0)

    def drain(ref, sem):
        part = ref.at[pl.ds(0, NSEQ - 1)]
        pltpu.make_async_copy(part, part, sem).wait()

    def arrived(src, dst, phase):
        pltpu.make_async_copy(src.at[me], dst.at[me], loc_sem.at[phase]).wait()
        drain(dst, recv_sem.at[phase])

    r32, c32 = iota((32, 32), 0), iota((32, 32), 1)
    mix32 = (c32 == (r32 % 2) * 16 + r32 // 2).astype(BF)

    def norm_step(i, _):
        dz = jnp.where(i == NZ - 1, 0, (i // 2) + 1)
        dz = jnp.where(i % 2 == 1, jnp.where(i == NZ - 1, 0, NZ - dz), dz)
        zz = (z + dz) % NZ
        f0 = pl.multiple_of(zz * XY, XY)
        parts = []
        for s in range(2):
            xf = xv[s, pl.ds(f0, XY), :].astype(F32)
            h = hcol[s, pl.ds(f0, XY), :]
            xf = jnp.where(h > 0.5, tok, xf)
            rinv = 1.0 / jnp.sqrt(jnp.mean(xf * xf, axis=1, keepdims=True) + 1e-06)
            rcol[s, pl.ds(f0, XY), :] = rinv
            parts.append((xf * rinv * gain).astype(BF))
        both = nn(mix32, jnp.concatenate(parts, axis=0)).astype(BF)
        xs[pl.ds(f0, XY)] = both.reshape(XY, 2, D)

        def body(k, _):
            to = zz * XY + ((y + k // 4) % 4) * 4 + (x + k % 4) % 4

            @pl.when(to != me)
            def _():
                send(xs.at[to], xr.at[me], 0, to).start()

            return 0

        lax.fori_loop(0, XY, body, 0)
        return 0

    lax.fori_loop(0, NZ, norm_step, 0)
    pltpu.make_async_copy(xs.at[me], xr.at[me], loc_sem.at[0]).start()

    ri, ci = iota((R, R), 0), iota((R, R), 1)
    mix = (ci == (ri % 2) * L + ri // 2).astype(BF)
    unmix = (ci == (ri % L) * 2 + ri // L).astype(BF)
    for c in load[4:6]:
        c.wait()

    @pl.loop(0, HW // 256)
    def _(n):
        n0 = pl.multiple_of(n * 256, 256)
        part = nt(cotv[...].reshape(R, D), wo[pl.ds(n0, 256), :]).astype(BF)
        tmp[:, pl.ds(n0, 256)] = nn(mix, part).astype(BF)

    gs[...] = tmp[:, :HW].reshape(NSEQ, 2, HW)
    send_all(gs, gr, 1)

    for c in load[6:9]:
        c.wait()
    clip_row = clipv[...]
    clip_col = to_column(clip_row, R)
    same = clip_col == clip_row
    first_row = jnp.min(jnp.where(same, ri, R), axis=0, keepdims=True)
    first_col = to_column(first_row, R)
    kind_col = to_column(kindv[...], R)
    joint_col = iota((R, 1), 0) - first_col
    pick = iota((R, JM), 1) == joint_col
    picked = jnp.zeros((R, JM), F32)
    for k in range(KINDS):
        rows = (pick & (kind_col == k)).astype(BF)
        picked = picked + nn(rows, adjv[k].astype(F32).astype(BF))
    link[...] = nt(pick.astype(BF), picked.astype(BF))
    neg[...] = jnp.where(same, jnp.float32(0.0), -jnp.inf)

    load[9].wait()
    arrived(xs, xr, 0)
    xn[...] = xr[...].reshape(R, D)

    @pl.loop(0, 3 * HW // 256)
    def _(n):
        n0 = pl.multiple_of(n * 256, 256)
        part = nn(xn[...], wq[:, pl.ds(n0, 256)]).astype(BF)
        scale = jnp.where(n < HW // 256, HD**-0.5, 1.0).astype(BF)
        qkv[:, pl.ds(n0, 256)] = part * scale

    coefs[...] = jnp.zeros_like(coefs)
    kt[...] = qkv[:, HW : 2 * HW].T
    vt[...] = qkv[:, 2 * HW :].T

    lane = iota((R, 128), 1)

    @pl.loop(0, PAIRS)
    def _(j):
        c0 = pl.multiple_of(j * 128, 128)
        q2 = qkv[:, pl.ds(c0, 128)]
        k2 = qkv[:, pl.ds(HW + c0, 128)]
        for i in range(2):
            h = j * 2 + i
            kh = jnp.where((lane < HD) == (i == 0), k2, jnp.zeros_like(k2))
            st = nt(kh, q2) + (coef_ref[h] * link[...] + neg[...])
            e = jnp.exp(st - jnp.max(st, axis=0, keepdims=True))
            pt = e * (1.0 / jnp.sum(e, axis=0, keepdims=True))
            pts[h] = pt
            r0 = pl.multiple_of(h * HD, HD)
            ctt[pl.ds(r0, HD), :] = nn(vt[pl.ds(r0, HD), :], pt.astype(BF)).astype(BF)

    cs[...] = ctt[...].T.reshape(NSEQ, 2, HW)
    send_all(cs, cr, 2)

    arrived(gs, gr, 1)
    gc[...] = gr[...].reshape(R, HW)

    @pl.loop(0, PAIRS)
    def _(j):
        c0 = pl.multiple_of(j * 128, 128)
        q2 = qkv[:, pl.ds(c0, 128)]
        v2 = qkv[:, pl.ds(2 * HW + c0, 128)]
        g2 = gc[:, pl.ds(c0, 128)]
        dk, dv = [], []
        for i in range(2):
            h = j * 2 + i
            vh = jnp.where((lane < HD) == (i == 0), v2, jnp.zeros_like(v2))
            dp = nt(vh, g2)
            pt = pts[h]
            ds = pt * (dp - jnp.sum(pt * dp, axis=0, keepdims=True))
            coefs[pl.ds(h, 1), :] = jnp.sum(ds * link[...], axis=0, keepdims=True)
            db = ds.astype(BF)
            r0 = pl.multiple_of(h * HD, HD)
            dq = nn(kt[pl.ds(r0, HD), :], db) * (HD**-0.5)
            ctt[pl.ds(r0, HD), :] = dq.astype(BF)
            dk.append(nn(db, q2))
            dv.append(nn(pt.astype(BF), g2))
        du[:, pl.ds(HW + c0, 128)] = jnp.where(lane < HD, dk[0], dk[1]).astype(BF)
        du[:, pl.ds(2 * HW + c0, 128)] = jnp.where(lane < HD, dv[0], dv[1]).astype(BF)

    du[:, :HW] = ctt[...].T

    @pl.loop(0, D // 256)
    def _(n):
        n0 = pl.multiple_of(n * 256, 256)
        tmp[:, pl.ds(n0, 256)] = nt(du[...], wq[pl.ds(n0, 256), :]).astype(BF)

    ns[...] = tmp[...].reshape(NSEQ, 2, D)
    send_all(ns, nr, 3)

    arrived(cs, cr, 2)
    gc[...] = nn(unmix, cr[...].reshape(R, HW)).astype(BF)

    @pl.loop(0, D // 256)
    def _(n):
        n0 = pl.multiple_of(n * 256, 256)
        part = nn(gc[...], wo[:, pl.ds(n0, 256)]).astype(BF).astype(F32)
        tokn = tokv[:, pl.ds(n0, 256)].astype(F32)
        for s in range(2):
            xf = jnp.where(hcol[s] > 0.5, tokn, xv[s, :, pl.ds(n0, 256)].astype(F32))
            outv[s, :, pl.ds(n0, 256)] = (xf + part[s * L : (s + 1) * L]).astype(BF)

    out_copy = pltpu.make_async_copy(outv, out_hbm.at[0], out_sem.at[0])
    out_copy.start()

    arrived(ns, nr, 3)
    xn[...] = nr[...].reshape(R, D)

    @pl.loop(0, D // 256)
    def _(n):
        n0 = pl.multiple_of(n * 256, 256)
        tmp[:, pl.ds(n0, 256)] = nn(unmix, xn[:, pl.ds(n0, 256)]).astype(BF)

    a0[...] = jnp.zeros_like(a0)

    def finish_step(i, sums):
        token_sum, gain_sum = sums
        s = i // 8
        f0 = pl.multiple_of((i % 8) * XY, XY)
        r0 = pl.multiple_of(i * XY, XY)
        h = hcol[s, pl.ds(f0, XY), :] > 0.5
        rinv = rcol[s, pl.ds(f0, XY), :]
        xu = jnp.where(h, tok, xv[s, pl.ds(f0, XY), :].astype(F32)) * rinv
        gn = tmp[pl.ds(r0, XY), :].astype(F32)
        g = gn * gain
        mean = jnp.mean(g * xu, axis=1, keepdims=True)
        gi = cotv[s, pl.ds(f0, XY), :].astype(F32) + (g - xu * mean) * rinv
        gxv[s, pl.ds(f0, XY), :] = jnp.where(h, 0.0, gi).astype(BF)
        ht = jnp.where(h, gi, 0.0)
        gx = gn * xu
        return token_sum + ht[:8] + ht[8:], gain_sum + gx[:8] + gx[8:]

    zero = jnp.zeros((8, D), F32)
    token_sum, gain_sum = lax.fori_loop(0, 16, finish_step, (zero, zero))
    gx_copy = pltpu.make_async_copy(gxv, gx_hbm.at[0], out_sem.at[1])
    gx_copy.start()
    token_sum = jnp.sum(token_sum, axis=0, keepdims=True)
    gain_sum = jnp.sum(gain_sum, axis=0, keepdims=True)
    coef_col = jnp.sum(coefs[...], axis=1, keepdims=True)
    coef_row = jnp.sum(
        jnp.where(iota((16, 128), 0) == iota((16, 128), 1), coef_col, 0.0), axis=0, keepdims=True
    )
    for c in range(12):
        a0[c // 2, pl.ds(c % 2, 1), :] = token_sum[:, c * 128 : (c + 1) * 128]
        a0[6 + c // 2, pl.ds(c % 2, 1), :] = gain_sum[:, c * 128 : (c + 1) * 128]
    a0[12, pl.ds(0, 1), :] = coef_row

    def small(src, dst, phase, to):
        return pltpu.make_async_remote_copy(
            src_ref=src,
            dst_ref=dst,
            send_sem=send_sem.at[phase],
            recv_sem=recv_sem.at[phase],
            device_id=to,
            device_id_type=MESH,
        )

    def drain15(ref, sem):
        part = ref.at[pl.ds(0, 15)]
        pltpu.make_async_copy(part, part, sem).wait()

    b1[pl.ds(yx, 1)] = a0[pl.ds(yx, 1)]

    def scatter(k, _):
        t = (yx + k) % XY
        small(a0.at[t], b1.at[yx], 4, {"seq": z * XY + t}).start()
        return 0

    lax.fori_loop(1, XY, scatter, 0)
    drain15(b1, recv_sem.at[4])
    zc = z * 2 + core
    b2[pl.ds(zc, 1)] = jnp.sum(b1[...], axis=0, keepdims=True)

    def across(k, _):
        t = (zc + k) % XY
        small(b2.at[zc], b2.at[zc], 5, {"dp": t % 2, "seq": (t // 2) * XY + yx}).start()
        return 0

    lax.fori_loop(1, XY, across, 0)
    drain15(b2, recv_sem.at[5])
    b3[pl.ds(yx, 1)] = jnp.sum(b2[...], axis=0, keepdims=True)

    def gather(k, _):
        t = (yx + k) % XY
        small(b3.at[yx], b3.at[yx], 6, {"seq": z * XY + t}).start()
        return 0

    lax.fori_loop(1, XY, gather, 0)
    drain15(b3, recv_sem.at[6])
    for c in range(12):
        token_ref[:, c * 128 : (c + 1) * 128] = b3[c // 2, pl.ds(c % 2, 1), :]
        gain_out_ref[:, c * 128 : (c + 1) * 128] = b3[6 + c // 2, pl.ds(c % 2, 1), :]
    coef_out_ref[...] = b3[12, pl.ds(0, 1), :]

    drain(xs, send_sem.at[0])
    drain(gs, send_sem.at[1])
    drain(cs, send_sem.at[2])
    drain(ns, send_sem.at[3])
    for phase, ref in ((4, a0), (5, b2), (6, b3)):
        drain15(ref, send_sem.at[phase])
    out_copy.wait()
    gx_copy.wait()


def on_device(
    joints_x,
    cotangent,
    hidden,
    stream_clip,
    stream_kind,
    adjacency,
    mask_token,
    norm_gain,
    w_qkv,
    w_out,
    graph_coef,
):
    any_space = pl.BlockSpec(memory_space=pl.ANY)
    vmem = pl.BlockSpec(memory_space=pltpu.VMEM)
    smem = pl.BlockSpec(memory_space=pltpu.SMEM)
    dma = pltpu.SemaphoreType.DMA
    S = jax.ShapeDtypeStruct
    outs = pl.pallas_call(
        fused_kernel,
        out_shape=(
            S((1, 2, L, D), BF),
            S((1, 2, L, D), BF),
            S((1, D), F32),
            S((1, D), F32),
            S((1, 128), F32),
        ),
        in_specs=[any_space] * 10 + [smem],
        out_specs=(any_space, any_space, vmem, vmem, vmem),
        scratch_shapes=[
            pltpu.VMEM((2, L, D), BF),
            pltpu.VMEM((2, L, D), BF),
            pltpu.VMEM((1, 2, L), jnp.int32),
            pltpu.VMEM((1, R), jnp.int32),
            pltpu.VMEM((1, R), jnp.int32),
            pltpu.VMEM((KINDS, JM, JM), jnp.int32),
            pltpu.VMEM((1, D), BF),
            pltpu.VMEM((1, D), F32),
            pltpu.VMEM((D, 3 * HW), BF),
            pltpu.VMEM((HW, D), BF),
            pltpu.VMEM((2, L, D), BF),
            pltpu.VMEM((2, L, D), BF),
            pltpu.VMEM((NSEQ, 2, D), BF),
            pltpu.VMEM((NSEQ, 2, D), BF),
            pltpu.VMEM((NSEQ, 2, HW), BF),
            pltpu.VMEM((NSEQ, 2, HW), BF),
            pltpu.VMEM((NSEQ, 2, HW), BF),
            pltpu.VMEM((NSEQ, 2, HW), BF),
            pltpu.VMEM((NSEQ, 2, D), BF),
            pltpu.VMEM((NSEQ, 2, D), BF),
            pltpu.VMEM((2, L, 1), F32),
            pltpu.VMEM((2, L, 1), F32),
            pltpu.VMEM((R, 3 * HW), BF),
            pltpu.VMEM((R, D), BF),
            pltpu.VMEM((R, HW), BF),
            pltpu.VMEM((HW, R), BF),
            pltpu.VMEM((HW, R), BF),
            pltpu.VMEM((HW, R), BF),
            pltpu.VMEM((HEADS, R, R), F32),
            pltpu.VMEM((R, 3 * HW), BF),
            pltpu.VMEM((R, R), F32),
            pltpu.VMEM((R, R), F32),
            pltpu.VMEM((16, R), F32),
            pltpu.VMEM((R, D), BF),
            pltpu.VMEM((16, 2, 128), F32),
            pltpu.VMEM((16, 2, 128), F32),
            pltpu.VMEM((16, 2, 128), F32),
            pltpu.VMEM((16, 2, 128), F32),
            dma((10,)),
            dma((7,)),
            dma((7,)),
            dma((4,)),
            dma((2,)),
        ],
        compiler_params=pltpu.CompilerParams(
            collective_id=0, has_side_effects=True, vmem_limit_bytes=60 << 20
        ),
    )(
        joints_x,
        cotangent,
        hidden,
        stream_clip,
        stream_kind,
        adjacency,
        mask_token.reshape(1, D),
        norm_gain.reshape(1, D),
        w_qkv,
        w_out,
        graph_coef,
    )
    layer_out, grad_x, token, gain, coef = outs
    return (layer_out, grad_x, token.reshape(D), gain.reshape(D), coef[0, :HEADS])


def solution(mesh):
    return jax.shard_map(
        on_device,
        mesh=mesh,
        in_specs=(
            P("dp", "seq", None, None),
            P("dp", "seq", None, None),
            P("dp", "seq", None),
            P("dp", None),
            P("dp", None),
            P(),
            P(),
            P(),
            P(),
            P(),
            P(),
        ),
        out_specs=(P("dp", "seq", None, None), P("dp", "seq", None, None), P(), P(), P()),
        check_vma=False,
    )
```

profile of v0, /device:TPU:1, one launch (start us, length us, event | category | flops | bytes accessed | tf_op | source)
XLA Modules:
  0.0 107.5 jit_solution(825117153789624560)
XLA Ops:
  0.6 1.3 %reshape.22.tok_hbm = bf16[1,1536]{1,0:T(2,128)(2,1)} reshape(bf16[1536]{0:T(1024)(128)(2,1)} %param.17) | data formatting | bytes 6144 | tf_op jit(solution)/shard_map/reshape | solution.py:524
  1.9 1.3 %reshape.23.gain_hbm = f32[1,1536]{1,0:T(1,128)} reshape(f32[1536]{0:T(1024)} %param.18) | data formatting | bytes 12288 | tf_op jit(solution)/shard_map/reshape | solution.py:525
  3.2 96.4 %shard_map.146 = (bf16[1,2,128,1536]{3,2,1,0:T(8,128)(2,1)}, bf16[1,2,128,1536]{3,2,1,0:T(8,128)(2,1)}, f32[1,1536]{1,0:T(1,128)}, f32[1,1536]{1,0:T(1,128)}, f32[1,128]{1,0:T(1,128)}) custom-call(bf16[1,2,128,1536]{3,2,1,0:T(8,128)(2,1)} %x_hbm.1, bf16[1,2,128,1536]{3,2,1,0:T(8,128)(2,1)} %cot_hbm.1, s32[1,2,128]{2,1,0:T(2,128)} %hid_hbm.1, ...), custom_call_target="tpu_custom_call" | custom-call | tf_op jit(solution)/shard_map/pallas_call | solution.py:458
  99.6 1.3 %reduce = f32[1536]{0:T(1024)} reduce(f32[1,1536]{1,0:T(1,128)} %get-tuple-element.12, f32[]{:T(128)} %constant.5), dimensions={0}, to_apply=%get-tuple-element.12.reduce_sub_computation | reduce | bytes 12292 | tf_op jit(solution)/shard_map/pallas_call | solution.py:458
  100.9 1.3 %reduce.1 = f32[1536]{0:T(1024)} reduce(f32[1,1536]{1,0:T(1,128)} %get-tuple-element.13, f32[]{:T(128)} %constant.5), dimensions={0}, to_apply=%get-tuple-element.13.reduce_sub_computation | reduce | bytes 12292 | tf_op jit(solution)/shard_map/pallas_call | solution.py:458
  102.2 1.1 %slice_bitcast_fusion = f32[12]{0:T(128)} fusion(f32[1,128]{1,0:T(1,128)} %get-tuple-element.14), kind=kLoop, calls=%fused_computation | loop fusion | bytes 96 | tf_op jit(solution)/shard_map/squeeze | solution.py:531
  103.4 2.1 %copy.18 = bf16[1,2,128,1536]{3,2,1,0:T(8,128)(2,1)} copy(bf16[1,2,128,1536]{3,2,1,0:T(8,128)(2,1)} %get-tuple-element.20) | data formatting | bytes 1572864
  105.4 2.1 %copy.19 = bf16[1,2,128,1536]{3,2,1,0:T(8,128)(2,1)} copy(bf16[1,2,128,1536]{3,2,1,0:T(8,128)(2,1)} %get-tuple-element.21) | data formatting | bytes 1572864
where the time goes:
time: 108 us; the launch traced here: 107 us
  Pallas kernels  96.4 us (89%)
  local copies, waits for them, and re-layouts  7.83 us (7%)
  other arithmetic  2.62 us (2%)
    pallas_call x1, Pallas kernels, on_device(): pl.pallas_call(fused_kernel, out_shape=(S((1, 2, L, D), BF), S((1, 2, L,...  96.4 us
    unnamed x2, local copies, waits for them, and re-layouts  4.12 us
    pallas_call x2, other arithmetic, on_device(): pl.pallas_call(fused_kernel, out_shape=(S((1, 2, L, D), BF), S((1, 2, L,...  2.62 us

commit v1 on v0

--- a/solution.py
+++ b/solution.py
@@ -22,6 +22,7 @@
 KINDS = 4
 JM = 136
 PAIRS = HEADS // 2
+MARK = 1000.0
 
 
 def iota(shape, axis):
@@ -53,8 +54,8 @@
     wqkv_hbm,
     wout_hbm,
     coef_ref,
-    out_hbm,
-    gx_hbm,
+    outv,
+    gxv,
     token_ref,
     gain_out_ref,
     coef_out_ref,
@@ -68,8 +69,6 @@
     gainv,
     wq,
     wo,
-    outv,
-    gxv,
     xs,
     xr,
     gs,
@@ -91,6 +90,7 @@
     link,
     neg,
     coefs,
+    sums,
     tmp,
     a0,
     b1,
@@ -100,7 +100,7 @@
     send_sem,
     recv_sem,
     loc_sem,
-    out_sem,
+    plane_sem,
 ):
     me = lax.axis_index("seq")
     core = lax.axis_index("dp")
@@ -153,8 +153,6 @@
     hid = hidv[0].astype(F32)
     for s in range(2):
         hcol[s] = to_column(hid[s : s + 1, :], L)
-    pl.semaphore_wait(barrier, NSEQ - 1 + NZ)
-
     def peer(dz, dyx):
         return ((z + dz) % NZ) * XY + ((y + dyx // 4) % 4) * 4 + (x + dyx % 4) % 4
 
@@ -189,10 +187,12 @@
     r32, c32 = iota((32, 32), 0), iota((32, 32), 1)
     mix32 = (c32 == (r32 % 2) * 16 + r32 // 2).astype(BF)
 
+    def offset(i):
+        near = i // 2 + 1
+        return jnp.where(i == NZ - 1, 0, jnp.where(i % 2 == 1, NZ - near, near))
+
     def norm_step(i, _):
-        dz = jnp.where(i == NZ - 1, 0, (i // 2) + 1)
-        dz = jnp.where(i % 2 == 1, jnp.where(i == NZ - 1, 0, NZ - dz), dz)
-        zz = (z + dz) % NZ
+        zz = (z + offset(i)) % NZ
         f0 = pl.multiple_of(zz * XY, XY)
         parts = []
         for s in range(2):
@@ -201,9 +201,15 @@
             xf = jnp.where(h > 0.5, tok, xf)
             rinv = 1.0 / jnp.sqrt(jnp.mean(xf * xf, axis=1, keepdims=True) + 1e-06)
             rcol[s, pl.ds(f0, XY), :] = rinv
-            parts.append((xf * rinv * gain).astype(BF))
+            row = xf * rinv * gain
+            mark = (h > 0.5) & (iota((XY, D), 1) == 0)
+            parts.append(jnp.where(mark, MARK, row).astype(BF))
         both = nn(mix32, jnp.concatenate(parts, axis=0)).astype(BF)
         xs[pl.ds(f0, XY)] = both.reshape(XY, 2, D)
+
+        @pl.when(i == 0)
+        def _():
+            pl.semaphore_wait(barrier, NSEQ - 1 + NZ)
 
         def body(k, _):
             to = zz * XY + ((y + k // 4) % 4) * 4 + (x + k % 4) % 4
@@ -223,6 +229,7 @@
     ri, ci = iota((R, R), 0), iota((R, R), 1)
     mix = (ci == (ri % 2) * L + ri // 2).astype(BF)
     unmix = (ci == (ri % L) * 2 + ri // L).astype(BF)
+    unmix32 = (c32 == (r32 % XY) * 2 + r32 // XY).astype(BF)
     for c in load[4:6]:
         c.wait()
 
@@ -233,6 +240,12 @@
         tmp[:, pl.ds(n0, 256)] = nn(mix, part).astype(BF)
 
     gs[...] = tmp[:, :HW].reshape(NSEQ, 2, HW)
+    scot = jnp.zeros((8, D), F32)
+    for s in range(2):
+        picks = jnp.broadcast_to(hid[s : s + 1, :], (8, L)).astype(BF)
+        scot = scot + nn(picks, cotv[s])
+    sums[0:1, :] = scot[0:1]
+    drain(xs, send_sem.at[0])
     send_all(gs, gr, 1)
 
     for c in load[6:9]:
@@ -255,6 +268,15 @@
     load[9].wait()
     arrived(xs, xr, 0)
     xn[...] = xr[...].reshape(R, D)
+    head = xn[:, :128]
+    flag_col = jnp.where(head[:, 0:1].astype(F32) > MARK / 2, 1.0, 0.0)
+    flag_row = jnp.sum(jnp.where(ri == ci, flag_col, 0.0), axis=0, keepdims=True)
+    flags = jnp.broadcast_to(flag_row, (8, R)).astype(BF)
+    tok_rinv = 1.0 / jnp.sqrt(jnp.mean(tok * tok, axis=1, keepdims=True) + 1e-06)
+    tok_unit = tok * tok_rinv
+    tok_head = (tok_unit * gain)[:, :128].astype(BF).astype(F32)
+    fix = (flag_col > 0.5) & (iota((R, 128), 1) == 0)
+    xn[:, :128] = jnp.where(fix, tok_head, head.astype(F32)).astype(BF)
 
     @pl.loop(0, 3 * HW // 256)
     def _(n):
@@ -318,63 +340,21 @@
     @pl.loop(0, D // 256)
     def _(n):
         n0 = pl.multiple_of(n * 256, 256)
-        tmp[:, pl.ds(n0, 256)] = nt(du[...], wq[pl.ds(n0, 256), :]).astype(BF)
-
-    ns[...] = tmp[...].reshape(NSEQ, 2, D)
-    send_all(ns, nr, 3)
-
-    arrived(cs, cr, 2)
-    gc[...] = nn(unmix, cr[...].reshape(R, HW)).astype(BF)
-
-    @pl.loop(0, D // 256)
-    def _(n):
-        n0 = pl.multiple_of(n * 256, 256)
-        part = nn(gc[...], wo[:, pl.ds(n0, 256)]).astype(BF).astype(F32)
-        tokn = tokv[:, pl.ds(n0, 256)].astype(F32)
-        for s in range(2):
-            xf = jnp.where(hcol[s] > 0.5, tokn, xv[s, :, pl.ds(n0, 256)].astype(F32))
-            outv[s, :, pl.ds(n0, 256)] = (xf + part[s * L : (s + 1) * L]).astype(BF)
-
-    out_copy = pltpu.make_async_copy(outv, out_hbm.at[0], out_sem.at[0])
-    out_copy.start()
-
-    arrived(ns, nr, 3)
-    xn[...] = nr[...].reshape(R, D)
-
-    @pl.loop(0, D // 256)
-    def _(n):
-        n0 = pl.multiple_of(n * 256, 256)
-        tmp[:, pl.ds(n0, 256)] = nn(unmix, xn[:, pl.ds(n0, 256)]).astype(BF)
-
-    a0[...] = jnp.zeros_like(a0)
-
-    def finish_step(i, sums):
-        token_sum, gain_sum = sums
-        s = i // 8
-        f0 = pl.multiple_of((i % 8) * XY, XY)
-        r0 = pl.multiple_of(i * XY, XY)
-        h = hcol[s, pl.ds(f0, XY), :] > 0.5
-        rinv = rcol[s, pl.ds(f0, XY), :]
-        xu = jnp.where(h, tok, xv[s, pl.ds(f0, XY), :].astype(F32)) * rinv
-        gn = tmp[pl.ds(r0, XY), :].astype(F32)
-        g = gn * gain
-        mean = jnp.mean(g * xu, axis=1, keepdims=True)
-        gi = cotv[s, pl.ds(f0, XY), :].astype(F32) + (g - xu * mean) * rinv
-        gxv[s, pl.ds(f0, XY), :] = jnp.where(h, 0.0, gi).astype(BF)
-        ht = jnp.where(h, gi, 0.0)
-        gx = gn * xu
-        return token_sum + ht[:8] + ht[8:], gain_sum + gx[:8] + gx[8:]
-
-    zero = jnp.zeros((8, D), F32)
-    token_sum, gain_sum = lax.fori_loop(0, 16, finish_step, (zero, zero))
-    gx_copy = pltpu.make_async_copy(gxv, gx_hbm.at[0], out_sem.at[1])
-    gx_copy.start()
-    token_sum = jnp.sum(token_sum, axis=0, keepdims=True)
-    gain_sum = jnp.sum(gain_sum, axis=0, keepdims=True)
+        gn = nt(du[...], wq[pl.ds(n0, 256), :]).astype(BF)
+        tmp[:, pl.ds(n0, 256)] = gn
+        sums[1:2, pl.ds(n0, 256)] = nn(flags, gn)[0:1]
+        prod = gn.astype(F32) * xn[:, pl.ds(n0, 256)].astype(F32)
+        sums[2:3, pl.ds(n0, 256)] = jnp.sum(prod, axis=0, keepdims=True)
+
+    sgn = gain * sums[1:2, :]
+    token_sum = sgn - tok_unit * jnp.mean(sgn * tok_unit, axis=1, keepdims=True)
+    token_sum = sums[0:1, :] + token_sum * tok_rinv
+    gain_sum = sums[2:3, :] / gain
     coef_col = jnp.sum(coefs[...], axis=1, keepdims=True)
     coef_row = jnp.sum(
         jnp.where(iota((16, 128), 0) == iota((16, 128), 1), coef_col, 0.0), axis=0, keepdims=True
     )
+    a0[...] = jnp.zeros_like(a0)
     for c in range(12):
         a0[c // 2, pl.ds(c % 2, 1), :] = token_sum[:, c * 128 : (c + 1) * 128]
         a0[6 + c // 2, pl.ds(c % 2, 1), :] = gain_sum[:, c * 128 : (c + 1) * 128]
@@ -402,6 +382,34 @@
         return 0
 
     lax.fori_loop(1, XY, scatter, 0)
+
+    ns[...] = tmp[...].reshape(NSEQ, 2, D)
+
+    def send_plane(i, _):
+        dz = offset(i)
+
+        def body(k, _):
+            to = peer(dz, k)
+
+            @pl.when(to != me)
+            def _():
+                pltpu.make_async_remote_copy(
+                    src_ref=ns.at[to],
+                    dst_ref=nr.at[me],
+                    send_sem=send_sem.at[3],
+                    recv_sem=plane_sem.at[dz],
+                    device_id={"seq": to},
+                    device_id_type=MESH,
+                ).start()
+
+            return 0
+
+        lax.fori_loop(0, XY, body, 0)
+        return 0
+
+    lax.fori_loop(0, NZ, send_plane, 0)
+    pltpu.make_async_copy(ns.at[me], nr.at[me], plane_sem.at[0]).start()
+
     drain15(b1, recv_sem.at[4])
     zc = z * 2 + core
     b2[pl.ds(zc, 1)] = jnp.sum(b1[...], axis=0, keepdims=True)
@@ -412,6 +420,19 @@
         return 0
 
     lax.fori_loop(1, XY, across, 0)
+
+    arrived(cs, cr, 2)
+    gc[...] = nn(unmix, cr[...].reshape(R, HW)).astype(BF)
+
+    @pl.loop(0, D // 256)
+    def _(n):
+        n0 = pl.multiple_of(n * 256, 256)
+        part = nn(gc[...], wo[:, pl.ds(n0, 256)]).astype(BF).astype(F32)
+        tokn = tokv[:, pl.ds(n0, 256)].astype(F32)
+        for s in range(2):
+            xf = jnp.where(hcol[s] > 0.5, tokn, xv[s, :, pl.ds(n0, 256)].astype(F32))
+            outv[0, s, :, pl.ds(n0, 256)] = (xf + part[s * L : (s + 1) * L]).astype(BF)
+
     drain15(b2, recv_sem.at[5])
     b3[pl.ds(yx, 1)] = jnp.sum(b2[...], axis=0, keepdims=True)
 
@@ -421,20 +442,50 @@
         return 0
 
     lax.fori_loop(1, XY, gather, 0)
+
+    def finish_step(i, _):
+        dz = offset(i)
+        f0 = pl.multiple_of(((z + NZ - dz) % NZ) * XY, XY)
+        block = nr.at[pl.ds(f0, XY)]
+        pltpu.make_async_copy(block, block, plane_sem.at[dz]).wait()
+        both = nn(unmix32, nr[pl.ds(f0, XY)].reshape(2 * XY, D))
+        for s in range(2):
+            h = hcol[s, pl.ds(f0, XY), :] > 0.5
+            rinv = rcol[s, pl.ds(f0, XY), :]
+            xu = jnp.where(h, tok, xv[s, pl.ds(f0, XY), :].astype(F32)) * rinv
+            g = both[s * XY : (s + 1) * XY] * gain
+            mean = jnp.mean(g * xu, axis=1, keepdims=True)
+            gi = cotv[s, pl.ds(f0, XY), :].astype(F32) + (g - xu * mean) * rinv
+            gxv[0, s, pl.ds(f0, XY), :] = jnp.where(h, 0.0, gi).astype(BF)
+        return 0
+
+    lax.fori_loop(0, NZ, finish_step, 0)
+
     drain15(b3, recv_sem.at[6])
     for c in range(12):
         token_ref[:, c * 128 : (c + 1) * 128] = b3[c // 2, pl.ds(c % 2, 1), :]
         gain_out_ref[:, c * 128 : (c + 1) * 128] = b3[6 + c // 2, pl.ds(c % 2, 1), :]
     coef_out_ref[...] = b3[12, pl.ds(0, 1), :]
 
-    drain(xs, send_sem.at[0])
     drain(gs, send_sem.at[1])
     drain(cs, send_sem.at[2])
     drain(ns, send_sem.at[3])
     for phase, ref in ((4, a0), (5, b2), (6, b3)):
         drain15(ref, send_sem.at[phase])
-    out_copy.wait()
-    gx_copy.wait()
+
+
+def place_kernel(out_in, gx_in, token_in, gain_in, coef_in, out, gx, token, gain, coef, sem):
+    copies = [
+        pltpu.make_async_copy(out_in, out, sem.at[0]),
+        pltpu.make_async_copy(gx_in, gx, sem.at[1]),
+    ]
+    for c in copies:
+        c.start()
+    token[...] = token_in[...].reshape(D)
+    gain[...] = gain_in[...].reshape(D)
+    coef[...] = coef_in[...].reshape(128)[:HEADS]
+    for c in copies:
+        c.wait()
 
 
 def on_device(
@@ -465,7 +516,7 @@
             S((1, 128), F32),
         ),
         in_specs=[any_space] * 10 + [smem],
-        out_specs=(any_space, any_space, vmem, vmem, vmem),
+        out_specs=(vmem,) * 5,
         scratch_shapes=[
             pltpu.VMEM((2, L, D), BF),
             pltpu.VMEM((2, L, D), BF),
@@ -477,8 +528,6 @@
             pltpu.VMEM((1, D), F32),
             pltpu.VMEM((D, 3 * HW), BF),
             pltpu.VMEM((HW, D), BF),
-            pltpu.VMEM((2, L, D), BF),
-            pltpu.VMEM((2, L, D), BF),
             pltpu.VMEM((NSEQ, 2, D), BF),
             pltpu.VMEM((NSEQ, 2, D), BF),
             pltpu.VMEM((NSEQ, 2, HW), BF),
@@ -500,6 +549,7 @@
             pltpu.VMEM((R, R), F32),
             pltpu.VMEM((R, R), F32),
             pltpu.VMEM((16, R), F32),
+            pltpu.VMEM((8, D), F32),
             pltpu.VMEM((R, D), BF),
             pltpu.VMEM((16, 2, 128), F32),
             pltpu.VMEM((16, 2, 128), F32),
@@ -509,7 +559,7 @@
             dma((7,)),
             dma((7,)),
             dma((4,)),
-            dma((2,)),
+            dma((NZ,)),
         ],
         compiler_params=pltpu.CompilerParams(
             collective_id=0, has_side_effects=True, vmem_limit_bytes=60 << 20
@@ -527,8 +577,19 @@
         w_out,
         graph_coef,
     )
-    layer_out, grad_x, token, gain, coef = outs
-    return (layer_out, grad_x, token.reshape(D), gain.reshape(D), coef[0, :HEADS])
+    return pl.pallas_call(
+        place_kernel,
+        out_shape=(
+            S((1, 2, L, D), BF),
+            S((1, 2, L, D), BF),
+            S((D,), F32),
+            S((D,), F32),
+            S((HEADS,), F32),
+        ),
+        in_specs=[vmem] * 5,
+        out_specs=(any_space, any_space, vmem, vmem, vmem),
+        scratch_shapes=[dma((2,))],
+    )(*outs)
 
 
 def solution(mesh):

time: 108 us -> 91.5 us (0.85)
  Pallas kernels: 96.4 us -> 88.1 us
  local copies, waits for them, and re-layouts: 7.83 us -> 2.58 us
  other arithmetic: 2.62 us -> 0 us
    pallas_call x1, Pallas kernels: 96.4 us -> 85 us  [on_device(): pl.pallas_call(fused_kernel, out_shape=(S((1, 2, L, D), BF), S((1, 2, L,...]
    unnamed x2 -> x0, local copies, waits for them, and re-layouts: 4.12 us -> none
    pallas_call x0 -> x1, Pallas kernels: none -> 3.15 us  [on_device(): pl.pallas_call(place_kernel, out_shape=(S((1, 2, L, D), BF), S((1, 2, L,...]
    pallas_call x2 -> x0, other arithmetic: 2.62 us -> none  [on_device(): pl.pallas_call(fused_kernel, out_shape=(S((1, 2, L, D), BF), S((1, 2, L,...]
    squeeze x1 -> x0, local copies, waits for them, and re-layouts: 1.13 us -> none  [on_device(): coef[0, :HEADS]]
where the time goes in v1:
time: 91.5 us; the launch traced here: 91.3 us
  Pallas kernels  88.1 us (96%)
  local copies, waits for them, and re-layouts  2.58 us (3%)
    pallas_call x1, Pallas kernels, on_device(): pl.pallas_call(fused_kernel, out_shape=(S((1, 2, L, D), BF), S((1, 2, L,...  85 us
    pallas_call x1, Pallas kernels, on_device(): pl.pallas_call(place_kernel, out_shape=(S((1, 2, L, D), BF), S((1, 2, L,...  3.15 us

profile of v1, /device:TPU:1, one launch (start us, length us, event | category | flops | bytes accessed | tf_op | source)
XLA Modules:
  0.0 91.3 jit_solution(6320551774902334968)
XLA Ops:
  0.6 1.3 %reshape.16.tok_hbm = bf16[1,1536]{1,0:T(2,128)(2,1)} reshape(bf16[1536]{0:T(1024)(128)(2,1)} %param.17) | data formatting | bytes 6144 | tf_op jit(solution)/shard_map/reshape | solution.py:574
  1.9 1.3 %reshape.17.gain_hbm = f32[1,1536]{1,0:T(1,128)} reshape(f32[1536]{0:T(1024)} %param.18) | data formatting | bytes 12288 | tf_op jit(solution)/shard_map/reshape | solution.py:575
  3.2 85.0 %shard_map.146 = (bf16[1,2,128,1536]{3,2,1,0:T(8,128)(2,1)}, bf16[1,2,128,1536]{3,2,1,0:T(8,128)(2,1)}, f32[1,1536]{1,0:T(1,128)}, f32[1,1536]{1,0:T(1,128)}, f32[1,128]{1,0:T(1,128)}) custom-call(bf16[1,2,128,1536]{3,2,1,0:T(8,128)(2,1)} %x_hbm.1, bf16[1,2,128,1536]{3,2,1,0:T(8,128)(2,1)} %cot_hbm.1, s32[1,2,128]{2,1,0:T(2,128)} %hid_hbm.1, ...), custom_call_target="tpu_custom_call" | custom-call | tf_op jit(solution)/shard_map/pallas_call | solution.py:509
  88.2 3.1 %shard_map.147 = (bf16[1,2,128,1536]{3,2,1,0:T(8,128)(2,1)}, bf16[1,2,128,1536]{3,2,1,0:T(8,128)(2,1)}, f32[1536]{0:T(1024)}, f32[1536]{0:T(1024)}, f32[12]{0:T(128)}) custom-call(bf16[1,2,128,1536]{3,2,1,0:T(8,128)(2,1)} %get-tuple-element.10.out_in, bf16[1,2,128,1536]{3,2,1,0:T(8,128)(2,1)} %get-tuple-element.11.gx_in, ...), custom_call_target="tpu_custom_call" | custom-call | tf_op jit(solution)/shard_map/pallas_call | solution.py:580

commit v2 on v1

--- a/solution.py
+++ b/solution.py
@@ -54,8 +54,8 @@
     wqkv_hbm,
     wout_hbm,
     coef_ref,
-    outv,
-    gxv,
+    out_hbm,
+    gx_hbm,
     token_ref,
     gain_out_ref,
     coef_out_ref,
@@ -69,6 +69,8 @@
     gainv,
     wq,
     wo,
+    outv,
+    gxv,
     xs,
     xr,
     gs,
@@ -77,6 +79,8 @@
     cr,
     ns,
     nr,
+    ns2,
+    nr2,
     hcol,
     rcol,
     qkv,
@@ -85,10 +89,12 @@
     vt,
     kt,
     ctt,
+    dqt,
     pts,
+    invs,
     du,
     link,
-    neg,
+    bias,
     coefs,
     sums,
     tmp,
@@ -101,6 +107,7 @@
     recv_sem,
     loc_sem,
     plane_sem,
+    out_sem,
 ):
     me = lax.axis_index("seq")
     core = lax.axis_index("dp")
@@ -148,8 +155,9 @@
 
     for c in load[:4]:
         c.wait()
-    tok = tokv[...].astype(F32)
-    gain = gainv[...]
+    tok = tokv[...].astype(F32).reshape(1, D)
+    gain = gainv[...].reshape(1, D)
+    sums[3:4, :] = tok
     hid = hidv[0].astype(F32)
     for s in range(2):
         hcol[s] = to_column(hid[s : s + 1, :], L)
@@ -233,7 +241,7 @@
     for c in load[4:6]:
         c.wait()
 
-    @pl.loop(0, HW // 256)
+    @pl.loop(0, HW // 256, unroll=True)
     def _(n):
         n0 = pl.multiple_of(n * 256, 256)
         part = nt(cotv[...].reshape(R, D), wo[pl.ds(n0, 256), :]).astype(BF)
@@ -263,7 +271,7 @@
         rows = (pick & (kind_col == k)).astype(BF)
         picked = picked + nn(rows, adjv[k].astype(F32).astype(BF))
     link[...] = nt(pick.astype(BF), picked.astype(BF))
-    neg[...] = jnp.where(same, jnp.float32(0.0), -jnp.inf)
+    bias[...] = jnp.where(same, link[...], -jnp.inf)
 
     load[9].wait()
     arrived(xs, xr, 0)
@@ -278,7 +286,7 @@
     fix = (flag_col > 0.5) & (iota((R, 128), 1) == 0)
     xn[:, :128] = jnp.where(fix, tok_head, head.astype(F32)).astype(BF)
 
-    @pl.loop(0, 3 * HW // 256)
+    @pl.loop(0, 3 * HW // 256, unroll=True)
     def _(n):
         n0 = pl.multiple_of(n * 256, 256)
         part = nn(xn[...], wq[:, pl.ds(n0, 256)]).astype(BF)
@@ -291,20 +299,27 @@
 
     lane = iota((R, 128), 1)
 
-    @pl.loop(0, PAIRS)
+    @pl.loop(0, PAIRS, unroll=True)
     def _(j):
         c0 = pl.multiple_of(j * 128, 128)
         q2 = qkv[:, pl.ds(c0, 128)]
         k2 = qkv[:, pl.ds(HW + c0, 128)]
         for i in range(2):
             h = j * 2 + i
+            r0 = pl.multiple_of(h * HD, HD)
             kh = jnp.where((lane < HD) == (i == 0), k2, jnp.zeros_like(k2))
-            st = nt(kh, q2) + (coef_ref[h] * link[...] + neg[...])
-            e = jnp.exp(st - jnp.max(st, axis=0, keepdims=True))
-            pt = e * (1.0 / jnp.sum(e, axis=0, keepdims=True))
-            pts[h] = pt
-            r0 = pl.multiple_of(h * HD, HD)
-            ctt[pl.ds(r0, HD), :] = nn(vt[pl.ds(r0, HD), :], pt.astype(BF)).astype(BF)
+            rows = []
+            for half in range(2):
+                cols = slice(half * 128, half * 128 + 128)
+                st = nt(kh, q2[cols]) + coef_ref[h] * bias[:, cols]
+                e = jnp.exp(st - jnp.max(st, axis=0, keepdims=True))
+                inv = 1.0 / jnp.sum(e, axis=0, keepdims=True)
+                eb = e.astype(BF)
+                pts[h, :, cols] = eb
+                rows.append(inv)
+                ct = nn(vt[pl.ds(r0, HD), :], eb) * inv
+                ctt[pl.ds(r0, HD), cols] = ct.astype(BF)
+            invs[pl.ds(h, 1), :] = jnp.concatenate(rows, axis=1)
 
     cs[...] = ctt[...].T.reshape(NSEQ, 2, HW)
     send_all(cs, cr, 2)
@@ -312,7 +327,7 @@
     arrived(gs, gr, 1)
     gc[...] = gr[...].reshape(R, HW)
 
-    @pl.loop(0, PAIRS)
+    @pl.loop(0, PAIRS, unroll=True)
     def _(j):
         c0 = pl.multiple_of(j * 128, 128)
         q2 = qkv[:, pl.ds(c0, 128)]
@@ -321,30 +336,66 @@
         dk, dv = [], []
         for i in range(2):
             h = j * 2 + i
+            r0 = pl.multiple_of(h * HD, HD)
             vh = jnp.where((lane < HD) == (i == 0), v2, jnp.zeros_like(v2))
-            dp = nt(vh, g2)
-            pt = pts[h]
-            ds = pt * (dp - jnp.sum(pt * dp, axis=0, keepdims=True))
-            coefs[pl.ds(h, 1), :] = jnp.sum(ds * link[...], axis=0, keepdims=True)
-            db = ds.astype(BF)
-            r0 = pl.multiple_of(h * HD, HD)
-            dq = nn(kt[pl.ds(r0, HD), :], db) * (HD**-0.5)
-            ctt[pl.ds(r0, HD), :] = dq.astype(BF)
-            dk.append(nn(db, q2))
-            dv.append(nn(pt.astype(BF), g2))
+            dbs, pbs, rows = [], [], []
+            inv = invs[pl.ds(h, 1), :]
+            for half in range(2):
+                cols = slice(half * 128, half * 128 + 128)
+                p = pts[h, :, cols].astype(F32) * inv[:, cols]
+                dp = nt(vh, g2[cols])
+                ds = p * (dp - jnp.sum(p * dp, axis=0, keepdims=True))
+                rows.append(jnp.sum(ds * link[:, cols], axis=0, keepdims=True))
+                db = ds.astype(BF)
+                dq = nn(kt[pl.ds(r0, HD), :], db) * (HD**-0.5)
+                dqt[pl.ds(r0, HD), cols] = dq.astype(BF)
+                dbs.append(db)
+                pbs.append(p.astype(BF))
+            coefs[pl.ds(h, 1), :] = jnp.concatenate(rows, axis=1)
+            dk.append(nn(jnp.concatenate(dbs, axis=1), q2))
+            dv.append(nn(jnp.concatenate(pbs, axis=1), g2))
         du[:, pl.ds(HW + c0, 128)] = jnp.where(lane < HD, dk[0], dk[1]).astype(BF)
         du[:, pl.ds(2 * HW + c0, 128)] = jnp.where(lane < HD, dv[0], dv[1]).astype(BF)
 
-    du[:, :HW] = ctt[...].T
-
-    @pl.loop(0, D // 256)
-    def _(n):
-        n0 = pl.multiple_of(n * 256, 256)
-        gn = nt(du[...], wq[pl.ds(n0, 256), :]).astype(BF)
-        tmp[:, pl.ds(n0, 256)] = gn
-        sums[1:2, pl.ds(n0, 256)] = nn(flags, gn)[0:1]
-        prod = gn.astype(F32) * xn[:, pl.ds(n0, 256)].astype(F32)
-        sums[2:3, pl.ds(n0, 256)] = jnp.sum(prod, axis=0, keepdims=True)
+    du[:, :HW] = dqt[...].T
+
+    for half, (src, dst) in enumerate(((ns, nr), (ns2, nr2))):
+
+        @pl.loop(0, HW // 256, unroll=True)
+        def _(n, half=half):
+            n0 = pl.multiple_of(half * HW + n * 256, 256)
+            gn = nt(du[...], wq[pl.ds(n0, 256), :]).astype(BF)
+            tmp[:, pl.ds(n0, 256)] = gn
+            sums[1:2, pl.ds(n0, 256)] = nn(flags, gn)[0:1]
+            prod = gn.astype(F32) * xn[:, pl.ds(n0, 256)].astype(F32)
+            sums[2:3, pl.ds(n0, 256)] = jnp.sum(prod, axis=0, keepdims=True)
+
+        src[...] = tmp[:, half * HW : half * HW + HW].reshape(NSEQ, 2, HW)
+
+        def send_plane(i, _, src=src, dst=dst, half=half):
+            dz = offset(i)
+
+            def body(k, _):
+                to = peer(dz, k)
+
+                @pl.when(to != me)
+                def _():
+                    pltpu.make_async_remote_copy(
+                        src_ref=src.at[to],
+                        dst_ref=dst.at[me],
+                        send_sem=send_sem.at[3 + half * 4],
+                        recv_sem=plane_sem.at[half, dz],
+                        device_id={"seq": to},
+                        device_id_type=MESH,
+                    ).start()
+
+                return 0
+
+            lax.fori_loop(0, XY, body, 0)
+            return 0
+
+        lax.fori_loop(0, NZ, send_plane, 0)
+        pltpu.make_async_copy(src.at[me], dst.at[me], plane_sem.at[half, 0]).start()
 
     sgn = gain * sums[1:2, :]
     token_sum = sgn - tok_unit * jnp.mean(sgn * tok_unit, axis=1, keepdims=True)
@@ -383,33 +434,6 @@
 
     lax.fori_loop(1, XY, scatter, 0)
 
-    ns[...] = tmp[...].reshape(NSEQ, 2, D)
-
-    def send_plane(i, _):
-        dz = offset(i)
-
-        def body(k, _):
-            to = peer(dz, k)
-
-            @pl.when(to != me)
-            def _():
-                pltpu.make_async_remote_copy(
-                    src_ref=ns.at[to],
-                    dst_ref=nr.at[me],
-                    send_sem=send_sem.at[3],
-                    recv_sem=plane_sem.at[dz],
-                    device_id={"seq": to},
-                    device_id_type=MESH,
-                ).start()
-
-            return 0
-
-        lax.fori_loop(0, XY, body, 0)
-        return 0
-
-    lax.fori_loop(0, NZ, send_plane, 0)
-    pltpu.make_async_copy(ns.at[me], nr.at[me], plane_sem.at[0]).start()
-
     drain15(b1, recv_sem.at[4])
     zc = z * 2 + core
     b2[pl.ds(zc, 1)] = jnp.sum(b1[...], axis=0, keepdims=True)
@@ -424,15 +448,17 @@
     arrived(cs, cr, 2)
     gc[...] = nn(unmix, cr[...].reshape(R, HW)).astype(BF)
 
-    @pl.loop(0, D // 256)
+    @pl.loop(0, D // 256, unroll=True)
     def _(n):
         n0 = pl.multiple_of(n * 256, 256)
         part = nn(gc[...], wo[:, pl.ds(n0, 256)]).astype(BF).astype(F32)
-        tokn = tokv[:, pl.ds(n0, 256)].astype(F32)
+        tokn = sums[3:4, pl.ds(n0, 256)]
         for s in range(2):
             xf = jnp.where(hcol[s] > 0.5, tokn, xv[s, :, pl.ds(n0, 256)].astype(F32))
-            outv[0, s, :, pl.ds(n0, 256)] = (xf + part[s * L : (s + 1) * L]).astype(BF)
-
+            outv[s, :, pl.ds(n0, 256)] = (xf + part[s * L : (s + 1) * L]).astype(BF)
+
+    out_copy = pltpu.make_async_copy(outv, out_hbm.at[0], out_sem.at[0])
+    out_copy.start()
     drain15(b2, recv_sem.at[5])
     b3[pl.ds(yx, 1)] = jnp.sum(b2[...], axis=0, keepdims=True)
 
@@ -446,9 +472,12 @@
     def finish_step(i, _):
         dz = offset(i)
         f0 = pl.multiple_of(((z + NZ - dz) % NZ) * XY, XY)
-        block = nr.at[pl.ds(f0, XY)]
-        pltpu.make_async_copy(block, block, plane_sem.at[dz]).wait()
-        both = nn(unmix32, nr[pl.ds(f0, XY)].reshape(2 * XY, D))
+        rows = []
+        for half, dst in enumerate((nr, nr2)):
+            block = dst.at[pl.ds(f0, XY)]
+            pltpu.make_async_copy(block, block, plane_sem.at[half, dz]).wait()
+            rows.append(dst[pl.ds(f0, XY)].reshape(2 * XY, HW))
+        both = nn(unmix32, jnp.concatenate(rows, axis=1))
         for s in range(2):
             h = hcol[s, pl.ds(f0, XY), :] > 0.5
             rinv = rcol[s, pl.ds(f0, XY), :]
@@ -456,7 +485,10 @@
             g = both[s * XY : (s + 1) * XY] * gain
             mean = jnp.mean(g * xu, axis=1, keepdims=True)
             gi = cotv[s, pl.ds(f0, XY), :].astype(F32) + (g - xu * mean) * rinv
-            gxv[0, s, pl.ds(f0, XY), :] = jnp.where(h, 0.0, gi).astype(BF)
+            gxv[s, pl.ds(f0, XY), :] = jnp.where(h, 0.0, gi).astype(BF)
+        pltpu.make_async_copy(
+            gxv.at[:, pl.ds(f0, XY)], gx_hbm.at[0, :, pl.ds(f0, XY)], out_sem.at[1]
+        ).start()
         return 0
 
     lax.fori_loop(0, NZ, finish_step, 0)
@@ -470,8 +502,11 @@
     drain(gs, send_sem.at[1])
     drain(cs, send_sem.at[2])
     drain(ns, send_sem.at[3])
+    drain(ns2, send_sem.at[7])
     for phase, ref in ((4, a0), (5, b2), (6, b3)):
         drain15(ref, send_sem.at[phase])
+    out_copy.wait()
+    pltpu.make_async_copy(gxv, gx_hbm.at[0], out_sem.at[1]).wait()
 
 
 def place_kernel(out_in, gx_in, token_in, gain_in, coef_in, out, gx, token, gain, coef, sem):
@@ -516,7 +551,7 @@
             S((1, 128), F32),
         ),
         in_specs=[any_space] * 10 + [smem],
-        out_specs=(vmem,) * 5,
+        out_specs=(any_space, any_space, vmem, vmem, vmem),
         scratch_shapes=[
             pltpu.VMEM((2, L, D), BF),
             pltpu.VMEM((2, L, D), BF),
@@ -524,18 +559,22 @@
             pltpu.VMEM((1, R), jnp.int32),
             pltpu.VMEM((1, R), jnp.int32),
             pltpu.VMEM((KINDS, JM, JM), jnp.int32),
-            pltpu.VMEM((1, D), BF),
-            pltpu.VMEM((1, D), F32),
+            pltpu.VMEM((D,), BF),
+            pltpu.VMEM((D,), F32),
             pltpu.VMEM((D, 3 * HW), BF),
             pltpu.VMEM((HW, D), BF),
+            pltpu.VMEM((2, L, D), BF),
+            pltpu.VMEM((2, L, D), BF),
             pltpu.VMEM((NSEQ, 2, D), BF),
             pltpu.VMEM((NSEQ, 2, D), BF),
             pltpu.VMEM((NSEQ, 2, HW), BF),
             pltpu.VMEM((NSEQ, 2, HW), BF),
             pltpu.VMEM((NSEQ, 2, HW), BF),
             pltpu.VMEM((NSEQ, 2, HW), BF),
-            pltpu.VMEM((NSEQ, 2, D), BF),
-            pltpu.VMEM((NSEQ, 2, D), BF),
+            pltpu.VMEM((NSEQ, 2, HW), BF),
+            pltpu.VMEM((NSEQ, 2, HW), BF),
+            pltpu.VMEM((NSEQ, 2, HW), BF),
+            pltpu.VMEM((NSEQ, 2, HW), BF),
             pltpu.VMEM((2, L, 1), F32),
             pltpu.VMEM((2, L, 1), F32),
             pltpu.VMEM((R, 3 * HW), BF),
@@ -544,7 +583,9 @@
             pltpu.VMEM((HW, R), BF),
             pltpu.VMEM((HW, R), BF),
             pltpu.VMEM((HW, R), BF),
-            pltpu.VMEM((HEADS, R, R), F32),
+            pltpu.VMEM((HW, R), BF),
+            pltpu.VMEM((HEADS, R, R), BF),
+            pltpu.VMEM((16, R), F32),
             pltpu.VMEM((R, 3 * HW), BF),
             pltpu.VMEM((R, R), F32),
             pltpu.VMEM((R, R), F32),
@@ -556,10 +597,11 @@
             pltpu.VMEM((16, 2, 128), F32),
             pltpu.VMEM((16, 2, 128), F32),
             dma((10,)),
-            dma((7,)),
+            dma((8,)),
             dma((7,)),
             dma((4,)),
-            dma((NZ,)),
+            dma((2, NZ)),
+            dma((2,)),
         ],
         compiler_params=pltpu.CompilerParams(
             collective_id=0, has_side_effects=True, vmem_limit_bytes=60 << 20
@@ -571,8 +613,8 @@
         stream_clip,
         stream_kind,
         adjacency,
-        mask_token.reshape(1, D),
-        norm_gain.reshape(1, D),
+        mask_token,
+        norm_gain,
         w_qkv,
         w_out,
         graph_coef,

time: 91.5 us -> 81.9 us (0.90)
  Pallas kernels: 88.1 us -> 81.2 us
  local copies, waits for them, and re-layouts: 2.58 us -> 0 us
    pallas_call x1, Pallas kernels: 85 us -> 78 us  [on_device(): pl.pallas_call(fused_kernel, out_shape=(S((1, 2, L, D), BF), S((1, 2, L,...]
    reshape x2 -> x0, local copies, waits for them, and re-layouts: 2.58 us -> none  [the longest x1 1.29 us: on_device(): norm_gain.reshape(1, D)]
where the time goes in v2:
time: 81.9 us; the launch traced here: 81.8 us
  Pallas kernels  81.2 us (99%)
    pallas_call x1, Pallas kernels, on_device(): pl.pallas_call(fused_kernel, out_shape=(S((1, 2, L, D), BF), S((1, 2, L,...  78 us
    pallas_call x1, Pallas kernels, on_device(): pl.pallas_call(place_kernel, out_shape=(S((1, 2, L, D), BF), S((1, 2, L,...  3.15 us

profile of v2, /device:TPU:1, one launch (start us, length us, event | category | flops | bytes accessed | tf_op | source)
XLA Modules:
  0.0 81.8 jit_solution(1094705494712416818)
XLA Ops:
  0.6 78.0 %shard_map.146 = (bf16[1,2,128,1536]{3,2,1,0:T(8,128)(2,1)}, bf16[1,2,128,1536]{3,2,1,0:T(8,128)(2,1)}, f32[1,1536]{1,0:T(1,128)}, f32[1,1536]{1,0:T(1,128)}, f32[1,128]{1,0:T(1,128)}) custom-call(bf16[1,2,128,1536]{3,2,1,0:T(8,128)(2,1)} %x_hbm.1, bf16[1,2,128,1536]{3,2,1,0:T(8,128)(2,1)} %cot_hbm.1, s32[1,2,128]{2,1,0:T(2,128)} %hid_hbm.1, ...), custom_call_target="tpu_custom_call" | custom-call | tf_op jit(solution)/shard_map/pallas_call | solution.py:544
  78.7 3.1 %shard_map.147 = (bf16[1,2,128,1536]{3,2,1,0:T(8,128)(2,1)}, bf16[1,2,128,1536]{3,2,1,0:T(8,128)(2,1)}, f32[1536]{0:T(1024)}, f32[1536]{0:T(1024)}, f32[12]{0:T(128)}) custom-call(bf16[1,2,128,1536]{3,2,1,0:T(8,128)(2,1)} %get-tuple-element.10.out_in, bf16[1,2,128,1536]{3,2,1,0:T(8,128)(2,1)} %get-tuple-element.11.gx_in, ...), custom_call_target="tpu_custom_call" | custom-call | tf_op jit(solution)/shard_map/pallas_call | solution.py:622

commit v3 on v2

--- a/solution.py
+++ b/solution.py
@@ -73,6 +73,9 @@
     gxv,
     xs,
     xr,
+    xs2,
+    xr2,
+    acc,
     gs,
     gr,
     cs,
@@ -213,7 +216,8 @@
             mark = (h > 0.5) & (iota((XY, D), 1) == 0)
             parts.append(jnp.where(mark, MARK, row).astype(BF))
         both = nn(mix32, jnp.concatenate(parts, axis=0)).astype(BF)
-        xs[pl.ds(f0, XY)] = both.reshape(XY, 2, D)
+        xs[pl.ds(f0, XY)] = both[:, :HW].reshape(XY, 2, HW)
+        xs2[pl.ds(f0, XY)] = both[:, HW:].reshape(XY, 2, HW)
 
         @pl.when(i == 0)
         def _():
@@ -233,6 +237,7 @@
 
     lax.fori_loop(0, NZ, norm_step, 0)
     pltpu.make_async_copy(xs.at[me], xr.at[me], loc_sem.at[0]).start()
+    send_all(xs2, xr2, 3)
 
     ri, ci = iota((R, R), 0), iota((R, R), 1)
     mix = (ci == (ri % 2) * L + ri // 2).astype(BF)
@@ -253,7 +258,6 @@
         picks = jnp.broadcast_to(hid[s : s + 1, :], (8, L)).astype(BF)
         scot = scot + nn(picks, cotv[s])
     sums[0:1, :] = scot[0:1]
-    drain(xs, send_sem.at[0])
     send_all(gs, gr, 1)
 
     for c in load[6:9]:
@@ -275,7 +279,7 @@
 
     load[9].wait()
     arrived(xs, xr, 0)
-    xn[...] = xr[...].reshape(R, D)
+    xn[:, :HW] = xr[...].reshape(R, HW)
     head = xn[:, :128]
     flag_col = jnp.where(head[:, 0:1].astype(F32) > MARK / 2, 1.0, 0.0)
     flag_row = jnp.sum(jnp.where(ri == ci, flag_col, 0.0), axis=0, keepdims=True)
@@ -289,7 +293,16 @@
     @pl.loop(0, 3 * HW // 256, unroll=True)
     def _(n):
         n0 = pl.multiple_of(n * 256, 256)
-        part = nn(xn[...], wq[:, pl.ds(n0, 256)]).astype(BF)
+        acc[:, pl.ds(n0, 256)] = nn(xn[:, :HW], wq[:HW, pl.ds(n0, 256)])
+
+    arrived(xs2, xr2, 3)
+    xn[:, HW:] = xr2[...].reshape(R, HW)
+
+    @pl.loop(0, 3 * HW // 256, unroll=True)
+    def _(n):
+        n0 = pl.multiple_of(n * 256, 256)
+        part = acc[:, pl.ds(n0, 256)] + nn(xn[:, HW:], wq[HW:, pl.ds(n0, 256)])
+        part = part.astype(BF)
         scale = jnp.where(n < HW // 256, HD**-0.5, 1.0).astype(BF)
         qkv[:, pl.ds(n0, 256)] = part * scale
 
@@ -315,7 +328,7 @@
                 e = jnp.exp(st - jnp.max(st, axis=0, keepdims=True))
                 inv = 1.0 / jnp.sum(e, axis=0, keepdims=True)
                 eb = e.astype(BF)
-                pts[h, :, cols] = eb
+                pts[h, :, cols] = e
                 rows.append(inv)
                 ct = nn(vt[pl.ds(r0, HD), :], eb) * inv
                 ctt[pl.ds(r0, HD), cols] = ct.astype(BF)
@@ -342,7 +355,7 @@
             inv = invs[pl.ds(h, 1), :]
             for half in range(2):
                 cols = slice(half * 128, half * 128 + 128)
-                p = pts[h, :, cols].astype(F32) * inv[:, cols]
+                p = pts[h, :, cols] * inv[:, cols]
                 dp = nt(vh, g2[cols])
                 ds = p * (dp - jnp.sum(p * dp, axis=0, keepdims=True))
                 rows.append(jnp.sum(ds * link[:, cols], axis=0, keepdims=True))
@@ -383,7 +396,7 @@
                     pltpu.make_async_remote_copy(
                         src_ref=src.at[to],
                         dst_ref=dst.at[me],
-                        send_sem=send_sem.at[3 + half * 4],
+                        send_sem=send_sem.at[8 - half],
                         recv_sem=plane_sem.at[half, dz],
                         device_id={"seq": to},
                         device_id_type=MESH,
@@ -499,9 +512,11 @@
         gain_out_ref[:, c * 128 : (c + 1) * 128] = b3[6 + c // 2, pl.ds(c % 2, 1), :]
     coef_out_ref[...] = b3[12, pl.ds(0, 1), :]
 
+    drain(xs, send_sem.at[0])
     drain(gs, send_sem.at[1])
     drain(cs, send_sem.at[2])
-    drain(ns, send_sem.at[3])
+    drain(xs2, send_sem.at[3])
+    drain(ns, send_sem.at[8])
     drain(ns2, send_sem.at[7])
     for phase, ref in ((4, a0), (5, b2), (6, b3)):
         drain15(ref, send_sem.at[phase])
@@ -565,8 +580,11 @@
             pltpu.VMEM((HW, D), BF),
             pltpu.VMEM((2, L, D), BF),
             pltpu.VMEM((2, L, D), BF),
-            pltpu.VMEM((NSEQ, 2, D), BF),
-            pltpu.VMEM((NSEQ, 2, D), BF),
+            pltpu.VMEM((NSEQ, 2, HW), BF),
+            pltpu.VMEM((NSEQ, 2, HW), BF),
+            pltpu.VMEM((NSEQ, 2, HW), BF),
+            pltpu.VMEM((NSEQ, 2, HW), BF),
+            pltpu.VMEM((R, 3 * HW), F32),
             pltpu.VMEM((NSEQ, 2, HW), BF),
             pltpu.VMEM((NSEQ, 2, HW), BF),
             pltpu.VMEM((NSEQ, 2, HW), BF),
@@ -584,7 +602,7 @@
             pltpu.VMEM((HW, R), BF),
             pltpu.VMEM((HW, R), BF),
             pltpu.VMEM((HW, R), BF),
-            pltpu.VMEM((HEADS, R, R), BF),
+            pltpu.VMEM((HEADS, R, R), F32),
             pltpu.VMEM((16, R), F32),
             pltpu.VMEM((R, 3 * HW), BF),
             pltpu.VMEM((R, R), F32),
@@ -597,7 +615,7 @@
             pltpu.VMEM((16, 2, 128), F32),
             pltpu.VMEM((16, 2, 128), F32),
             dma((10,)),
-            dma((8,)),
+            dma((9,)),
             dma((7,)),
             dma((4,)),
             dma((2, NZ)),

time: 81.9 us -> 81.2 us (level)
  no operation moved by 1% of the time
where the time goes in v3:
time: 81.2 us; the launch traced here: 81.1 us
  Pallas kernels  80.4 us (99%)
    pallas_call x1, Pallas kernels, on_device(): pl.pallas_call(fused_kernel, out_shape=(S((1, 2, L, D), BF), S((1, 2, L,...  77.3 us
    pallas_call x1, Pallas kernels, on_device(): pl.pallas_call(place_kernel, out_shape=(S((1, 2, L, D), BF), S((1, 2, L,...  3.15 us

profile of v3, /device:TPU:1, one launch (start us, length us, event | category | flops | bytes accessed | tf_op | source)
XLA Modules:
  0.0 81.1 jit_solution(4132974465385924738)
XLA Ops:
  0.6 77.3 %shard_map.146 = (bf16[1,2,128,1536]{3,2,1,0:T(8,128)(2,1)}, bf16[1,2,128,1536]{3,2,1,0:T(8,128)(2,1)}, f32[1,1536]{1,0:T(1,128)}, f32[1,1536]{1,0:T(1,128)}, f32[1,128]{1,0:T(1,128)}) custom-call(bf16[1,2,128,1536]{3,2,1,0:T(8,128)(2,1)} %x_hbm.1, bf16[1,2,128,1536]{3,2,1,0:T(8,128)(2,1)} %cot_hbm.1, s32[1,2,128]{2,1,0:T(2,128)} %hid_hbm.1, ...), custom_call_target="tpu_custom_call" | custom-call | tf_op jit(solution)/shard_map/pallas_call | solution.py:559
  77.9 3.1 %shard_map.147 = (bf16[1,2,128,1536]{3,2,1,0:T(8,128)(2,1)}, bf16[1,2,128,1536]{3,2,1,0:T(8,128)(2,1)}, f32[1536]{0:T(1024)}, f32[1536]{0:T(1024)}, f32[12]{0:T(128)}) custom-call(bf16[1,2,128,1536]{3,2,1,0:T(8,128)(2,1)} %get-tuple-element.10.out_in, bf16[1,2,128,1536]{3,2,1,0:T(8,128)(2,1)} %get-tuple-element.11.gx_in, ...), custom_call_target="tpu_custom_call" | custom-call | tf_op jit(solution)/shard_map/pallas_call | solution.py:640
